TPU v7x, 32 devices: a whole 2x2x4 slice. The times are simulated.
32 devices in a mesh: row: 4 (over x, core), col: 2 (over y), layer: 4 (over z).
Axes of the slice: x: 2, y: 2, z: 4, core: 2. Of those that a mesh axis runs over, the one named last changes fastest.
Arguments:
- density_matrix: bfloat16 [2048, 2048], P('row', 'col'), may hold values from -3 to 3
- block_mask: int32 [32, 32], P('row', 'col'), may hold values 0 or 1
- intersection_weights: float32 [2048], P(('col', 'layer')), may hold values from -0.125 to 0.125
- exponents: float32 [2048], P('row'), may hold values from 0.5 to 8
- anchor_x: int32 [32], P('row'), may hold values from 0 to 31
- anchor_y: int32 [32], P('row'), may hold values from 0 to 127, as said below
- anchor_z: int32 [32], P('row'), may hold values from 0 to 127
Outputs:
- squared: bfloat16 [2048, 2048], P('row', ('col', 'layer'))
- density: float32 [128, 128, 128], P('row', ('col', 'layer'))
Inputs may be any that keep to these rules, and one draw needn't show every extreme that they name: `anchor_y`: block row a starts in the second dimension between (a mod (8)) * 16 and that plus 16 - 1.
All inputs are finite; a program needn't handle non-finite values. No bound on the sum of `block_mask` on one device may be relied on, other than what follows from the above.
Results may differ from a plain program's by a relative error of at most 0.0055.
Values may be sent and summed in bfloat16 or wider, within the bound.
A program may use at most 64 MiB of HBM per device.

v0:
```python
import jax
import jax.numpy as jnp
from jax import lax
from jax.sharding import PartitionSpec as P

BLOCK = 64
TILE = 16
SX = 32
SY = 16
GZ = 128
grid_step_sq = 0.0625


def broadcast(block, axis, source):
    block = jnp.where(lax.axis_index(axis) == source, block, jnp.zeros_like(block))
    return lax.psum(block, axis)


def shifted(block, axis, distance):
    devices = range(lax.axis_size(axis))
    route = [((i - distance) % len(devices), i) for i in devices]
    return lax.ppermute(block, axis, route)


def local(
    density_matrix, block_mask, intersection_weights, exponents, anchor_x, anchor_y, anchor_z
):
    row_count = lax.axis_size("row")
    col_count = lax.axis_size("col")
    layer_count = lax.axis_size("layer")
    rows_here = density_matrix.shape[0]
    cols_here = density_matrix.shape[1]
    col_ratio = row_count // col_count
    layer_at = lax.axis_index("layer")
    wide_mask = jnp.repeat(jnp.repeat(block_mask, BLOCK, 0), BLOCK, 1)
    masked = jnp.where(wide_mask > 0, density_matrix, jnp.zeros_like(density_matrix))
    width = cols_here // layer_count
    own_cols = lax.dynamic_slice_in_dim(masked, layer_at * width, width, 1)
    running = jnp.zeros((rows_here, width), jnp.float32)
    for inner_at in range(row_count):
        left_part = lax.dynamic_slice_in_dim(masked, inner_at % col_ratio * rows_here, rows_here, 1)
        left_part = broadcast(left_part, "col", inner_at // col_ratio)
        right_part = broadcast(own_cols, "row", inner_at)
        running = running + jnp.dot(left_part, right_part, preferred_element_type=jnp.float32)
    squared = running.astype(jnp.bfloat16)
    partial_charges = jnp.dot(running, intersection_weights, precision=lax.Precision.HIGHEST)
    charges = lax.psum(partial_charges, ("col", "layer"))
    atom_count = anchor_x.shape[0]
    y_index = lax.axis_index("col") * layer_count + layer_at
    offsets = jnp.arange(TILE, dtype=jnp.int32)
    centre = offsets.astype(jnp.float32) - 7.5
    atom_charges = charges.reshape(atom_count, BLOCK)
    decay_rates = exponents.reshape(atom_count, BLOCK)
    profiles = jnp.exp(-decay_rates[:, :, None] * grid_step_sq * centre[None, None, :] ** 2)
    all_tiles = jnp.einsum(
        "ak,akx,aky,akz->axyz",
        atom_charges,
        profiles,
        profiles,
        profiles,
        precision=lax.Precision.HIGHEST,
    )

    def deposit(atom_at, buffer):
        start_y = anchor_y[atom_at] - y_index * SY
        is_owned = (start_y >= 0) & (start_y < SY)
        start_y = jnp.where(is_owned, start_y, 0)
        weight = jnp.where(is_owned, 1.0, 0.0).astype(jnp.float32)
        tile_values = lax.dynamic_index_in_dim(all_tiles, atom_at, 0, keepdims=False)
        start_x = anchor_x[atom_at]
        start_z = anchor_z[atom_at]
        current = lax.dynamic_slice(buffer, (start_x, start_y, start_z), (TILE, TILE, TILE))
        return lax.dynamic_update_slice(
            buffer, current + weight * tile_values, (start_x, start_y, start_z)
        )

    buffer = lax.fori_loop(
        0, atom_count, deposit, jnp.zeros((SX + TILE, SY + TILE, GZ + TILE), jnp.float32)
    )
    buffer = buffer[:, :, :GZ].at[:, :, :TILE].add(buffer[:, :, GZ:])
    rim_x = buffer[SX:]
    came_x = shifted(rim_x.astype(jnp.bfloat16), "row", 1).astype(rim_x.dtype)
    base = buffer[:SX].at[:TILE].add(came_x)
    rim_y = base[:, SY:]
    came_y = shifted(rim_y.astype(jnp.bfloat16), ("col", "layer"), 1).astype(rim_y.dtype)
    density = base[:, :SY].at[:, :TILE].add(came_y)
    return (squared, density)


def solution(mesh):
    return jax.shard_map(
        local,
        mesh=mesh,
        in_specs=(
            P("row", "col"),
            P("row", "col"),
            P(("col", "layer")),
            P("row"),
            P("row"),
            P("row"),
            P("row"),
        ),
        out_specs=(P("row", ("col", "layer")), P("row", ("col", "layer"), None)),
        check_vma=False,
    )
```

profile of v0, /device:TPU:0, one launch (start us, length us, event | category | flops | bytes accessed | tf_op | source)
XLA Modules:
  0.0 261.5 jit_solution(14411166556518656421)
XLA Ops:
  7.2 1.5 copy.11
  9.2 1.1 broadcast_select_fusion.4
  10.3 1.4 broadcast_select_fusion
  11.7 0.6 copy-done.7
  12.5 37.8 %all-reduce.5.cloned.1.call-done = (bf16[512,256]{0,1:T(8,128)(2,1)}, bf16[512,256]{0,1:T(8,128)(2,1)}, bf16[512,256]{0,1:T(8,128)(2,1)}, bf16[512,256]{0,1:T(8,128)(2,1)}) async-done(((bf16[512,256]{0,1:T(8,128)(2,1)}, bf16[512,256]{0,1:T(8,128)(2,1)}, bf16[512,256]{0,1:T(8,128)(2,1)}, bf16[512,256]{0,1:T(8,128)(2,1)}), (bf16[512,256]{0,1:T(8,128)(2,1)}, bf16[512,256]{0,1:T(8,128)(2,1)}, ...) | async-done | bytes 1048592 | tf_op jit(solution)/shard_map/psum | solution.py:16
  50.3 66.0 %all-reduce.7.cloned.1.call-done = (bf16[512,512]{0,1:T(8,128)(2,1)}, bf16[512,512]{0,1:T(8,128)(2,1)}, bf16[512,512]{0,1:T(8,128)(2,1)}, bf16[512,512]{0,1:T(8,128)(2,1)}) async-done(((bf16[512,512]{0,1:T(8,128)(2,1)}, bf16[512,512]{0,1:T(8,128)(2,1)}, bf16[512,512]{0,1:T(8,128)(2,1)}, bf16[512,512]{0,1:T(8,128)(2,1)}), (bf16[512,512]{0,1:T(8,128)(2,1)}, bf16[512,512]{0,1:T(8,128)(2,1)}, ...) | async-done | bytes 2097168 | tf_op jit(solution)/shard_map/psum | solution.py:16
  116.3 1.6 fusion.8
  117.9 1.4 convolution_add_fusion.2
  119.3 0.3 convolution_add_fusion.1
  119.7 1.0 fusion.7
  120.7 0.5 fusion.9
  121.4 20.6 %psum.71 = f32[8,64]{1,0:T(8,128)S(1)} all-reduce(f32[8,64]{1,0:T(8,128)S(1)} %reshape.127), channel_id=1, replica_groups=mesh['row'=4,'col'=2,'layer'=4] {'col','layer'}, use_global_device_ids=true, to_apply=%region_8.9 | all-reduce | flops 512 | bytes 4096 | tf_op jit(solution)/shard_map/psum | solution.py:47
  141.9 1.1 convolution_bitcast_fusion
  143.0 0.2 broadcast_in_dim.16
  143.2 96.2 %while.19 = (s32[]{:T(128)}, f32[48,32,144]{2,1,0:T(8,128)S(1)}, s32[8]{0:T(128)S(1)}, s32[8]{0:T(128)S(1)}, s32[]{:T(128)}, /*index=5*/s32[8]{0:T(128)S(1)}, f3...) while((s32[]{:T(128)}, f32[48,32,144]{2,1,0:T(8,128)S(1)}, ...), condition=%wide.region_10.11_spmd, body=%wide.region_9.10_spmd.sunk | while | flops 8209 | bytes 147826 | solution.py:77
  143.2 0.1 copy.16
  143.4 0.6 dynamic_slice.79
  145.9 0.6 dynamic_slice.80
  147.2 0.6 dynamic_slice.81
  149.7 0.1 bitcast_add_fusion.2
  149.8 5.4 %dynamic_update_slice.10 = f32[48,32,144]{2,1,0:T(8,128)S(1)} dynamic-update-slice(f32[48,32,144]{2,1,0:T(8,128)S(1)} %get-tuple-element.322, f32[16,16,16]{2,1,0:T(8,128)S(1)} %bitcast_add_fusion.2, s32[]{:T(128)S(6)} %select_n.154, s32[]{:T(128)S(6)} %select_n.156, s32[]{:T(128)S(6)} %select_n.157) | dynamic-update-slice | bytes 32772 | tf_op jit(solution)/shard_map/while/body/eval_jaxpr/dynamic_update_slice | solution.py:73
  155.3 0.1 copy.16
  155.4 0.6 dynamic_slice.79
  157.9 0.6 dynamic_slice.80
  159.2 0.6 dynamic_slice.81
  161.7 0.1 bitcast_add_fusion.2
  161.8 5.4 %dynamic_update_slice.10 = f32[48,32,144]{2,1,0:T(8,128)S(1)} dynamic-update-slice(f32[48,32,144]{2,1,0:T(8,128)S(1)} %get-tuple-element.322, f32[16,16,16]{2,1,0:T(8,128)S(1)} %bitcast_add_fusion.2, s32[]{:T(128)S(6)} %select_n.154, s32[]{:T(128)S(6)} %select_n.156, s32[]{:T(128)S(6)} %select_n.157) | dynamic-update-slice | bytes 32772 | tf_op jit(solution)/shard_map/while/body/eval_jaxpr/dynamic_update_slice | solution.py:73
  167.3 0.1 copy.16
  167.4 0.6 dynamic_slice.79
  169.9 0.6 dynamic_slice.80
  171.2 0.6 dynamic_slice.81
  173.7 0.1 bitcast_add_fusion.2
  173.9 5.4 %dynamic_update_slice.10 = f32[48,32,144]{2,1,0:T(8,128)S(1)} dynamic-update-slice(f32[48,32,144]{2,1,0:T(8,128)S(1)} %get-tuple-element.322, f32[16,16,16]{2,1,0:T(8,128)S(1)} %bitcast_add_fusion.2, s32[]{:T(128)S(6)} %select_n.154, s32[]{:T(128)S(6)} %select_n.156, s32[]{:T(128)S(6)} %select_n.157) | dynamic-update-slice | bytes 32772 | tf_op jit(solution)/shard_map/while/body/eval_jaxpr/dynamic_update_slice | solution.py:73
  179.3 0.1 copy.16
  179.4 0.6 dynamic_slice.79
  182.0 0.6 dynamic_slice.80
  183.2 0.6 dynamic_slice.81
  185.8 0.1 bitcast_add_fusion.2
  185.9 5.4 %dynamic_update_slice.10 = f32[48,32,144]{2,1,0:T(8,128)S(1)} dynamic-update-slice(f32[48,32,144]{2,1,0:T(8,128)S(1)} %get-tuple-element.322, f32[16,16,16]{2,1,0:T(8,128)S(1)} %bitcast_add_fusion.2, s32[]{:T(128)S(6)} %select_n.154, s32[]{:T(128)S(6)} %select_n.156, s32[]{:T(128)S(6)} %select_n.157) | dynamic-update-slice | bytes 32772 | tf_op jit(solution)/shard_map/while/body/eval_jaxpr/dynamic_update_slice | solution.py:73
  191.3 0.1 copy.16
  191.5 0.6 dynamic_slice.79
  194.0 0.6 dynamic_slice.80
  195.2 0.6 dynamic_slice.81
  197.8 0.1 bitcast_add_fusion.2
  197.9 5.4 %dynamic_update_slice.10 = f32[48,32,144]{2,1,0:T(8,128)S(1)} dynamic-update-slice(f32[48,32,144]{2,1,0:T(8,128)S(1)} %get-tuple-element.322, f32[16,16,16]{2,1,0:T(8,128)S(1)} %bitcast_add_fusion.2, s32[]{:T(128)S(6)} %select_n.154, s32[]{:T(128)S(6)} %select_n.156, s32[]{:T(128)S(6)} %select_n.157) | dynamic-update-slice | bytes 32772 | tf_op jit(solution)/shard_map/while/body/eval_jaxpr/dynamic_update_slice | solution.py:73
  203.3 0.1 copy.16
  203.5 0.6 dynamic_slice.79
  206.0 0.6 dynamic_slice.80
  207.3 0.6 dynamic_slice.81
  209.9 5.4 %dynamic_update_slice.10 = f32[48,32,144]{2,1,0:T(8,128)S(1)} dynamic-update-slice(f32[48,32,144]{2,1,0:T(8,128)S(1)} %get-tuple-element.322, f32[16,16,16]{2,1,0:T(8,128)S(1)} %bitcast_add_fusion.2, s32[]{:T(128)S(6)} %select_n.154, s32[]{:T(128)S(6)} %select_n.156, s32[]{:T(128)S(6)} %select_n.157) | dynamic-update-slice | bytes 32772 | tf_op jit(solution)/shard_map/while/body/eval_jaxpr/dynamic_update_slice | solution.py:73
  215.4 0.1 copy.16
  215.5 0.6 dynamic_slice.79
  218.0 0.6 dynamic_slice.80
  219.3 0.6 dynamic_slice.81
  221.9 5.4 %dynamic_update_slice.10 = f32[48,32,144]{2,1,0:T(8,128)S(1)} dynamic-update-slice(f32[48,32,144]{2,1,0:T(8,128)S(1)} %get-tuple-element.322, f32[16,16,16]{2,1,0:T(8,128)S(1)} %bitcast_add_fusion.2, s32[]{:T(128)S(6)} %select_n.154, s32[]{:T(128)S(6)} %select_n.156, s32[]{:T(128)S(6)} %select_n.157) | dynamic-update-slice | bytes 32772 | tf_op jit(solution)/shard_map/while/body/eval_jaxpr/dynamic_update_slice | solution.py:73
  227.4 0.1 copy.16
  227.5 0.6 dynamic_slice.79
  230.1 0.6 dynamic_slice.80
  231.3 0.6 dynamic_slice.81
  234.0 5.4 %dynamic_update_slice.10 = f32[48,32,144]{2,1,0:T(8,128)S(1)} dynamic-update-slice(f32[48,32,144]{2,1,0:T(8,128)S(1)} %get-tuple-element.322, f32[16,16,16]{2,1,0:T(8,128)S(1)} %bitcast_add_fusion.2, s32[]{:T(128)S(6)} %select_n.154, s32[]{:T(128)S(6)} %select_n.156, s32[]{:T(128)S(6)} %select_n.157) | dynamic-update-slice | bytes 32772 | tf_op jit(solution)/shard_map/while/body/eval_jaxpr/dynamic_update_slice | solution.py:73
  239.6 2.0 scatter-add.6
  241.8 4.3 %collective-permute-done = bf16[16,32,128]{2,1,0:T(8,128)(2,1)S(1)} collective-permute-done((bf16[16,32,128]{2,1,0:T(8,128)(2,1)S(1)}, bf16[16,32,128]{2,1,0:T(8,128)(2,1)S(1)}, u32[]{:S(2)}, u32[]{:S(2)}) %collective-permute-start) | collective-permute-done | bytes 131104 | tf_op jit(solution)/shard_map/ppermute | solution.py:22
  246.2 7.7 %collective-permute-done.1 = bf16[32,16,128]{2,1,0:T(8,128)(2,1)S(1)} collective-permute-done((bf16[32,16,128]{2,1,0:T(8,128)(2,1)S(1)}, bf16[32,16,128]{2,1,0:T(8,128)(2,1)S(1)}, u32[]{:S(2)}, u32[]{:S(2)}) %collective-permute-start.1) | collective-permute-done | bytes 131104 | tf_op jit(solution)/shard_map/ppermute | solution.py:22
  253.9 0.7 slice_add_fusion.1
  (54 shorter events, 1.6 us)
Async XLA Ops:
  7.2 113.6 %copy-start = (f32[256]{0:T(256)S(1)}, f32[256]{0:T(256)}, u32[]{:S(2)}) copy-start(f32[256]{0:T(256)} %param.19) | copy-start | bytes 3076
  7.2 1.6 copy-start.6
  7.2 43.1 %all-reduce.5.cloned.1.call-start = ((), (), s32[]{:S(2)}) async-start(), calls=%async_computation | async-start | bytes 2097152 | tf_op jit(solution)/shard_map/psum | solution.py:16
  10.2 106.1 %all-reduce.7.cloned.1.call-start = ((), (), s32[]{:S(2)}) async-start(), calls=%async_computation.1 | async-start | bytes 4194304 | tf_op jit(solution)/shard_map/psum | solution.py:16
  11.7 0.7 copy-start.7
  116.3 1.6 copy-start.2
  116.3 3.0 %copy-start.1 = (bf16[512,512]{0,1:T(8,128)(2,1)S(1)}, bf16[512,512]{0,1:T(8,128)(2,1)}, u32[]{:S(2)}) copy-start(bf16[512,512]{0,1:T(8,128)(2,1)} %get-tuple-element.251) | copy-start | bytes 1572868
  116.3 3.0 %copy-start.4 = (bf16[512,256]{0,1:T(8,128)(2,1)S(1)}, bf16[512,256]{0,1:T(8,128)(2,1)}, u32[]{:S(2)}) copy-start(bf16[512,256]{0,1:T(8,128)(2,1)} %get-tuple-element.247) | copy-start | bytes 786436
  117.9 1.8 copy-start.3
  117.9 1.8 copy-start.5
  120.7 22.4 %copy-start.8 = (s32[8]{0:T(128)S(1)}, s32[8]{0:T(128)}, u32[]{:S(2)}) copy-start(s32[8]{0:T(128)} %param.21) | copy-start | bytes 100
  120.7 22.4 %copy-start.9 = (s32[8]{0:T(128)S(1)}, s32[8]{0:T(128)}, u32[]{:S(2)}) copy-start(s32[8]{0:T(128)} %param.22) | copy-start | bytes 100
  120.7 22.5 %copy-start.10 = (s32[8]{0:T(128)S(1)}, s32[8]{0:T(128)}, u32[]{:S(2)}) copy-start(s32[8]{0:T(128)} %param.23) | copy-start | bytes 100
  241.7 4.4 %collective-permute-start = (bf16[16,32,128]{2,1,0:T(8,128)(2,1)S(1)}, bf16[16,32,128]{2,1,0:T(8,128)(2,1)S(1)}, u32[]{:S(2)}, u32[]{:S(2)}) collective-permute-start(bf16[16,32,128]{2,1,0:T(8,128)(2,1)S(1)} %slice.111), channel_id=1, source_target_pairs={{24,0},{0,8},{8,16},{16,24},{25,1},{1,9},{9,17},{17,25},{26,2},{2,... | collective-permute-start | bytes 393224 | tf_op jit(solution)/shard_map/ppermute | solution.py:22
  246.2 7.7 %collective-permute-start.1 = (bf16[32,16,128]{2,1,0:T(8,128)(2,1)S(1)}, bf16[32,16,128]{2,1,0:T(8,128)(2,1)S(1)}, u32[]{:S(2)}, u32[]{:S(2)}) collective-permute-start(bf16[32,16,128]{2,1,0:T(8,128)(2,1)S(1)} %slice.110), channel_id=1, source_target_pairs={{7,0},{0,1},{1,2},{2,3},{3,4},{4,5},{5,6},{6,7},{15,8},{8,9},{9,10... | collective-permute-start | bytes 393224 | tf_op jit(solution)/shard_map/ppermute | solution.py:22
Sparse Core Ops, SparseCore 0:
  11.1 39.1 all-reduce.4
  52.8 63.5 all-reduce.6
where the time goes:
time: 262 us; the launch traced here: 261 us
  waiting for transfers between devices  116 us (44%)
  local copies, waits for them, and re-layouts  63.4 us (24%)
  loops' own time  36.8 us (14%)
  blocking collectives  20.6 us (8%)
  between operations  14.3 us (5%)
  matrix products  5.91 us (2%)
  other arithmetic  4.43 us (2%)
    psum x2, waiting for transfers between devices, broadcast(): return lax.psum(block, axis)  104 us
    dynamic_update_slice x8, local copies, waits for them, and re-layouts, deposit(): lax.dynamic_update_slice(buffer, current + weight * tile_values, (start_x...  43.1 us
    another operation x1, loops' own time, local(): lax.fori_loop(0, atom_count, deposit, jnp.zeros((SX + TILE, SY + TILE, GZ...  36.8 us
    psum x1, blocking collectives, local(): charges = lax.psum(partial_charges, ('col', 'layer'))  20.6 us
    ppermute x2, waiting for transfers between devices, shifted(): return lax.ppermute(block, axis, route)  12 us
  transfers between devices with their start and end apart: 4, of which 4 were waited for; matrix products, arithmetic and copies ran while one was open for 1% of the time, Pallas kernels for 0%

commit v1 on v0

--- a/solution.py
+++ b/solution.py
@@ -44,7 +44,7 @@
         running = running + jnp.dot(left_part, right_part, preferred_element_type=jnp.float32)
     squared = running.astype(jnp.bfloat16)
     partial_charges = jnp.dot(running, intersection_weights, precision=lax.Precision.HIGHEST)
-    charges = lax.psum(partial_charges, ("col", "layer"))
+    charges = jnp.sum(lax.all_gather(partial_charges, ("col", "layer")), axis=0)
     atom_count = anchor_x.shape[0]
     y_index = lax.axis_index("col") * layer_count + layer_at
     offsets = jnp.arange(TILE, dtype=jnp.int32)

time: 262 us -> 269 us (1.027)
  blocking collectives: 20.6 us -> 27 us
    all_gather x0 -> x1, blocking collectives: none -> 27 us  [local(): charges = jnp.sum(lax.all_gather(partial_charges, ('col', 'layer')), axis=0)]
    psum x1 -> x0, blocking collectives: 20.6 us -> none  [local(): charges = lax.psum(partial_charges, ('col', 'layer'))]
where the time goes in v1:
time: 269 us; the launch traced here: 268 us
  waiting for transfers between devices  115 us (43%)
  local copies, waits for them, and re-layouts  63.4 us (24%)
  loops' own time  36.8 us (14%)
  blocking collectives  27 us (10%)
  between operations  14.3 us (5%)
  matrix products  5.91 us (2%)
  other arithmetic  4.46 us (2%)
    psum x2, waiting for transfers between devices, broadcast(): return lax.psum(block, axis)  104 us
    dynamic_update_slice x8, local copies, waits for them, and re-layouts, deposit(): lax.dynamic_update_slice(buffer, current + weight * tile_values, (start_x...  43.1 us
    another operation x1, loops' own time, local(): lax.fori_loop(0, atom_count, deposit, jnp.zeros((SX + TILE, SY + TILE, GZ...  36.8 us
    all_gather x1, blocking collectives, local(): charges = jnp.sum(lax.all_gather(partial_charges, ('col', 'layer')), axis=0)  27 us
    ppermute x2, waiting for transfers between devices, shifted(): return lax.ppermute(block, axis, route)  11.4 us
  transfers between devices with their start and end apart: 4, of which 4 were waited for; matrix products, arithmetic and copies ran while one was open for 1% of the time, Pallas kernels for 0%

profile of v1, /device:TPU:0, one launch (start us, length us, event | category | flops | bytes accessed | tf_op | source)
XLA Modules:
  0.0 268.0 jit_solution(16348250379827280773)
XLA Ops:
  7.2 1.5 copy.14
  9.2 1.1 broadcast_select_fusion.4
  10.3 1.4 broadcast_select_fusion
  11.7 0.6 copy-done.7
  12.5 37.8 %all-reduce.5.cloned.1.call-done = (bf16[512,256]{0,1:T(8,128)(2,1)}, bf16[512,256]{0,1:T(8,128)(2,1)}, bf16[512,256]{0,1:T(8,128)(2,1)}, bf16[512,256]{0,1:T(8,128)(2,1)}) async-done(((bf16[512,256]{0,1:T(8,128)(2,1)}, bf16[512,256]{0,1:T(8,128)(2,1)}, bf16[512,256]{0,1:T(8,128)(2,1)}, bf16[512,256]{0,1:T(8,128)(2,1)}), (bf16[512,256]{0,1:T(8,128)(2,1)}, bf16[512,256]{0,1:T(8,128)(2,1)}, ...) | async-done | bytes 1048592 | tf_op jit(solution)/shard_map/psum | solution.py:16
  50.3 66.0 %all-reduce.7.cloned.1.call-done = (bf16[512,512]{0,1:T(8,128)(2,1)}, bf16[512,512]{0,1:T(8,128)(2,1)}, bf16[512,512]{0,1:T(8,128)(2,1)}, bf16[512,512]{0,1:T(8,128)(2,1)}) async-done(((bf16[512,512]{0,1:T(8,128)(2,1)}, bf16[512,512]{0,1:T(8,128)(2,1)}, bf16[512,512]{0,1:T(8,128)(2,1)}, bf16[512,512]{0,1:T(8,128)(2,1)}), (bf16[512,512]{0,1:T(8,128)(2,1)}, bf16[512,512]{0,1:T(8,128)(2,1)}, ...) | async-done | bytes 2097168 | tf_op jit(solution)/shard_map/psum | solution.py:16
  116.3 1.6 fusion.8
  117.9 1.4 convolution_add_fusion.2
  119.3 0.3 convolution_add_fusion.1
  119.7 1.0 fusion.7
  120.7 0.5 convolution_bitcast_fusion.1
  121.3 27.0 %all-gather.1 = f32[8,1,512]{2,1,0:T(1,128)S(1)} all-gather(f32[1,1,512]{2,1,0:T(1,128)S(1)} %convolution_bitcast_fusion.1), channel_id=2, replica_groups=mesh['row'=4,'col'=2,'layer'=4] {'col','layer'}, dimensions={0}, use_global_device_ids=true | all-gather | bytes 18432 | tf_op jit(solution)/shard_map/all_gather | solution.py:47
  148.4 1.1 convolution_bitcast_fusion
  149.5 0.2 broadcast_in_dim.16
  149.7 96.2 %while.19 = (s32[]{:T(128)}, f32[48,32,144]{2,1,0:T(8,128)S(1)}, s32[8]{0:T(128)S(1)}, s32[8]{0:T(128)S(1)}, s32[]{:T(128)}, /*index=5*/s32[8]{0:T(128)S(1)}, f3...) while((s32[]{:T(128)}, f32[48,32,144]{2,1,0:T(8,128)S(1)}, ...), condition=%wide.region_10.11_spmd, body=%wide.region_9.10_spmd.sunk | while | flops 8209 | bytes 147826 | solution.py:77
  149.7 0.1 copy.19
  149.9 0.6 dynamic_slice.79
  152.4 0.6 dynamic_slice.80
  153.7 0.6 dynamic_slice.81
  156.2 0.1 bitcast_add_fusion.2
  156.3 5.4 %dynamic_update_slice.10 = f32[48,32,144]{2,1,0:T(8,128)S(1)} dynamic-update-slice(f32[48,32,144]{2,1,0:T(8,128)S(1)} %get-tuple-element.329, f32[16,16,16]{2,1,0:T(8,128)S(1)} %bitcast_add_fusion.2, s32[]{:T(128)S(6)} %select_n.154, s32[]{:T(128)S(6)} %select_n.156, s32[]{:T(128)S(6)} %select_n.157) | dynamic-update-slice | bytes 32772 | tf_op jit(solution)/shard_map/while/body/eval_jaxpr/dynamic_update_slice | solution.py:73
  161.8 0.1 copy.19
  161.9 0.6 dynamic_slice.79
  164.4 0.6 dynamic_slice.80
  165.7 0.6 dynamic_slice.81
  168.2 0.1 bitcast_add_fusion.2
  168.4 5.4 %dynamic_update_slice.10 = f32[48,32,144]{2,1,0:T(8,128)S(1)} dynamic-update-slice(f32[48,32,144]{2,1,0:T(8,128)S(1)} %get-tuple-element.329, f32[16,16,16]{2,1,0:T(8,128)S(1)} %bitcast_add_fusion.2, s32[]{:T(128)S(6)} %select_n.154, s32[]{:T(128)S(6)} %select_n.156, s32[]{:T(128)S(6)} %select_n.157) | dynamic-update-slice | bytes 32772 | tf_op jit(solution)/shard_map/while/body/eval_jaxpr/dynamic_update_slice | solution.py:73
  173.8 0.1 copy.19
  173.9 0.6 dynamic_slice.79
  176.5 0.6 dynamic_slice.80
  177.7 0.6 dynamic_slice.81
  180.3 0.1 bitcast_add_fusion.2
  180.4 5.4 %dynamic_update_slice.10 = f32[48,32,144]{2,1,0:T(8,128)S(1)} dynamic-update-slice(f32[48,32,144]{2,1,0:T(8,128)S(1)} %get-tuple-element.329, f32[16,16,16]{2,1,0:T(8,128)S(1)} %bitcast_add_fusion.2, s32[]{:T(128)S(6)} %select_n.154, s32[]{:T(128)S(6)} %select_n.156, s32[]{:T(128)S(6)} %select_n.157) | dynamic-update-slice | bytes 32772 | tf_op jit(solution)/shard_map/while/body/eval_jaxpr/dynamic_update_slice | solution.py:73
  185.8 0.1 copy.19
  185.9 0.6 dynamic_slice.79
  188.5 0.6 dynamic_slice.80
  189.7 0.6 dynamic_slice.81
  192.3 0.1 bitcast_add_fusion.2
  192.4 5.4 %dynamic_update_slice.10 = f32[48,32,144]{2,1,0:T(8,128)S(1)} dynamic-update-slice(f32[48,32,144]{2,1,0:T(8,128)S(1)} %get-tuple-element.329, f32[16,16,16]{2,1,0:T(8,128)S(1)} %bitcast_add_fusion.2, s32[]{:T(128)S(6)} %select_n.154, s32[]{:T(128)S(6)} %select_n.156, s32[]{:T(128)S(6)} %select_n.157) | dynamic-update-slice | bytes 32772 | tf_op jit(solution)/shard_map/while/body/eval_jaxpr/dynamic_update_slice | solution.py:73
  197.8 0.1 copy.19
  198.0 0.6 dynamic_slice.79
  200.5 0.6 dynamic_slice.80
  201.8 0.6 dynamic_slice.81
  204.4 5.4 %dynamic_update_slice.10 = f32[48,32,144]{2,1,0:T(8,128)S(1)} dynamic-update-slice(f32[48,32,144]{2,1,0:T(8,128)S(1)} %get-tuple-element.329, f32[16,16,16]{2,1,0:T(8,128)S(1)} %bitcast_add_fusion.2, s32[]{:T(128)S(6)} %select_n.154, s32[]{:T(128)S(6)} %select_n.156, s32[]{:T(128)S(6)} %select_n.157) | dynamic-update-slice | bytes 32772 | tf_op jit(solution)/shard_map/while/body/eval_jaxpr/dynamic_update_slice | solution.py:73
  209.9 0.1 copy.19
  210.0 0.6 dynamic_slice.79
  212.5 0.6 dynamic_slice.80
  213.8 0.6 dynamic_slice.81
  216.4 5.4 %dynamic_update_slice.10 = f32[48,32,144]{2,1,0:T(8,128)S(1)} dynamic-update-slice(f32[48,32,144]{2,1,0:T(8,128)S(1)} %get-tuple-element.329, f32[16,16,16]{2,1,0:T(8,128)S(1)} %bitcast_add_fusion.2, s32[]{:T(128)S(6)} %select_n.154, s32[]{:T(128)S(6)} %select_n.156, s32[]{:T(128)S(6)} %select_n.157) | dynamic-update-slice | bytes 32772 | tf_op jit(solution)/shard_map/while/body/eval_jaxpr/dynamic_update_slice | solution.py:73
  221.9 0.1 copy.19
  222.0 0.6 dynamic_slice.79
  224.5 0.6 dynamic_slice.80
  225.8 0.6 dynamic_slice.81
  228.5 5.4 %dynamic_update_slice.10 = f32[48,32,144]{2,1,0:T(8,128)S(1)} dynamic-update-slice(f32[48,32,144]{2,1,0:T(8,128)S(1)} %get-tuple-element.329, f32[16,16,16]{2,1,0:T(8,128)S(1)} %bitcast_add_fusion.2, s32[]{:T(128)S(6)} %select_n.154, s32[]{:T(128)S(6)} %select_n.156, s32[]{:T(128)S(6)} %select_n.157) | dynamic-update-slice | bytes 32772 | tf_op jit(solution)/shard_map/while/body/eval_jaxpr/dynamic_update_slice | solution.py:73
  233.9 0.1 copy.19
  234.0 0.6 dynamic_slice.79
  236.6 0.6 dynamic_slice.80
  237.8 0.6 dynamic_slice.81
  240.5 5.4 %dynamic_update_slice.10 = f32[48,32,144]{2,1,0:T(8,128)S(1)} dynamic-update-slice(f32[48,32,144]{2,1,0:T(8,128)S(1)} %get-tuple-element.329, f32[16,16,16]{2,1,0:T(8,128)S(1)} %bitcast_add_fusion.2, s32[]{:T(128)S(6)} %select_n.154, s32[]{:T(128)S(6)} %select_n.156, s32[]{:T(128)S(6)} %select_n.157) | dynamic-update-slice | bytes 32772 | tf_op jit(solution)/shard_map/while/body/eval_jaxpr/dynamic_update_slice | solution.py:73
  246.1 2.0 scatter-add.6
  248.3 4.3 %collective-permute-done = bf16[16,32,128]{2,1,0:T(8,128)(2,1)S(1)} collective-permute-done((bf16[16,32,128]{2,1,0:T(8,128)(2,1)S(1)}, bf16[16,32,128]{2,1,0:T(8,128)(2,1)S(1)}, u32[]{:S(2)}, u32[]{:S(2)}) %collective-permute-start) | collective-permute-done | bytes 131104 | tf_op jit(solution)/shard_map/ppermute | solution.py:22
  252.7 0.6 collective-permute-start.1
  253.3 7.1 %collective-permute-done.1 = bf16[32,16,128]{2,1,0:T(8,128)(2,1)S(1)} collective-permute-done((bf16[32,16,128]{2,1,0:T(8,128)(2,1)S(1)}, bf16[32,16,128]{2,1,0:T(8,128)(2,1)S(1)}, u32[]{:S(2)}, u32[]{:S(2)}) %collective-permute-start.1) | collective-permute-done | bytes 131104 | tf_op jit(solution)/shard_map/ppermute | solution.py:22
  260.4 0.7 slice_add_fusion.1
  (55 shorter events, 1.7 us)
Async XLA Ops:
  7.2 113.6 %copy-start = (f32[256]{0:T(256)S(1)}, f32[256]{0:T(256)}, u32[]{:S(2)}) copy-start(f32[256]{0:T(256)} %param.19) | copy-start | bytes 3076
  7.2 1.6 copy-start.6
  7.2 43.1 %all-reduce.5.cloned.1.call-start = ((), (), s32[]{:S(2)}) async-start(), calls=%async_computation | async-start | bytes 2097152 | tf_op jit(solution)/shard_map/psum | solution.py:16
  10.2 106.1 %all-reduce.7.cloned.1.call-start = ((), (), s32[]{:S(2)}) async-start(), calls=%async_computation.1 | async-start | bytes 4194304 | tf_op jit(solution)/shard_map/psum | solution.py:16
  11.7 0.7 copy-start.7
  116.3 1.6 copy-start.2
  116.3 3.0 %copy-start.1 = (bf16[512,512]{0,1:T(8,128)(2,1)S(1)}, bf16[512,512]{0,1:T(8,128)(2,1)}, u32[]{:S(2)}) copy-start(bf16[512,512]{0,1:T(8,128)(2,1)} %get-tuple-element.258) | copy-start | bytes 1572868
  116.3 3.0 %copy-start.4 = (bf16[512,256]{0,1:T(8,128)(2,1)S(1)}, bf16[512,256]{0,1:T(8,128)(2,1)}, u32[]{:S(2)}) copy-start(bf16[512,256]{0,1:T(8,128)(2,1)} %get-tuple-element.254) | copy-start | bytes 786436
  117.9 1.8 copy-start.3
  117.9 1.8 copy-start.5
  120.7 28.9 %copy-start.8 = (s32[8]{0:T(128)S(1)}, s32[8]{0:T(128)}, u32[]{:S(2)}) copy-start(s32[8]{0:T(128)} %param.21) | copy-start | bytes 100
  120.7 29.0 %copy-start.9 = (s32[8]{0:T(128)S(1)}, s32[8]{0:T(128)}, u32[]{:S(2)}) copy-start(s32[8]{0:T(128)} %param.22) | copy-start | bytes 100
  120.7 29.0 %copy-start.10 = (s32[8]{0:T(128)S(1)}, s32[8]{0:T(128)}, u32[]{:S(2)}) copy-start(s32[8]{0:T(128)} %param.23) | copy-start | bytes 100
  248.2 4.4 %collective-permute-start = (bf16[16,32,128]{2,1,0:T(8,128)(2,1)S(1)}, bf16[16,32,128]{2,1,0:T(8,128)(2,1)S(1)}, u32[]{:S(2)}, u32[]{:S(2)}) collective-permute-start(bf16[16,32,128]{2,1,0:T(8,128)(2,1)S(1)} %slice.111), channel_id=1, source_target_pairs={{24,0},{0,8},{8,16},{16,24},{25,1},{1,9},{9,17},{17,25},{26,2},{2,... | collective-permute-start | bytes 393224 | tf_op jit(solution)/shard_map/ppermute | solution.py:22
  252.7 7.7 %collective-permute-start.1 = (bf16[32,16,128]{2,1,0:T(8,128)(2,1)S(1)}, bf16[32,16,128]{2,1,0:T(8,128)(2,1)S(1)}, u32[]{:S(2)}, u32[]{:S(2)}) collective-permute-start(bf16[32,16,128]{2,1,0:T(8,128)(2,1)S(1)} %slice.110), channel_id=1, source_target_pairs={{7,0},{0,1},{1,2},{2,3},{3,4},{4,5},{5,6},{6,7},{15,8},{8,9},{9,10... | collective-permute-start | bytes 393224 | tf_op jit(solution)/shard_map/ppermute | solution.py:22
Sparse Core Ops, SparseCore 0:
  11.1 39.1 all-reduce.4
  52.8 63.5 all-reduce.6
